TPU v7x, 512 devices: a whole 4x4x16 slice. The times are simulated.
512 devices in a mesh: dp: 2 (over z_hi), row: 8 (over y, core), col: 32 (over x, z_lo).
Axes of the slice: x: 4, y: 4, z: 16 (z_hi: 2, z_lo: 8; z = z_hi * 8 + z_lo), core: 2. Of those that a mesh axis runs over, the one named last changes fastest.
Arguments:
- activations: bfloat16 [2048, 16384], P(('dp', 'row'), 'col'), may hold values from -6 to 6
- cotangent: bfloat16 [2048, 16384], P(('dp', 'row'), 'col'), may hold values from -6 to 6
- gate_saved: bfloat16 [2048, 6656], P(('dp', 'col'), 'row'), may hold values from -6 to 6
- up_saved: bfloat16 [2048, 6656], P(('dp', 'col'), 'row'), may hold values from -6 to 6
- w_gate: bfloat16 [16384, 6656], P('col', 'row'), may hold values from -0.046875 to 0.046875
- w_up: bfloat16 [16384, 6656], P('col', 'row'), may hold values from -0.046875 to 0.046875
- w_down: bfloat16 [6656, 16384], P('row', 'col'), may hold values from -0.078125 to 0.078125
- assignment: int32 [4], replicated, may hold values from 0 to 3, each once
- pair_lengths: int32 [8], replicated, may hold values from 1 to 256, 1536 in all
Outputs:
- input_grad: bfloat16 [2048, 16384], P(('dp', 'row'), 'col')
- gate_grad: bfloat16 [16384, 6656], P(('col', 'dp'), 'row')
- up_grad: bfloat16 [16384, 6656], P(('col', 'dp'), 'row')
- down_grad: bfloat16 [6656, 16384], P(('row', 'dp'), 'col')
Inputs may be any that keep to these rules, and one draw needn't show every extreme that they name: `assignment`: each of the 4 pairs stands in exactly one pair slot; pair slot s belongs to batch s // 2. `pair_lengths`: entry 2 p is the live length of pair p's chosen sequence and entry 2 p + 1 that of its rejected one; the largest entry is exactly 256.
All inputs are finite; a program needn't handle non-finite values.
Results may differ from a plain program's by a relative error of at most 0.019.
Values may be sent and summed in bfloat16 or wider, within the bound.
No kernel may reach another device: no remote copies, remote signals or barrier semaphores. Data moves between devices by JAX's collectives and lax.ppermute only.
A program may use at most 64 MiB of HBM per device.

v0:
```python
import jax
import jax.numpy as jnp
from jax import lax
from jax.sharding import PartitionSpec as P

SEQ = 256


def contract_last(left, right):
    return lax.dot_general(
        left, right, (((1,), (1,)), ((), ())), preferred_element_type=jnp.float32
    )


def contract_first(left, right):
    return lax.dot_general(
        left, right, (((0,), (0,)), ((), ())), preferred_element_type=jnp.float32
    )


def live_mask(assignment, pair_lengths, batch_id, row_count):
    seq_count = row_count // SEQ
    seq_index = jnp.arange(seq_count, dtype=jnp.int32)
    slot_ids = batch_id * (seq_count // 2) + seq_index // 2
    slot_table = jnp.arange(assignment.shape[0], dtype=jnp.int32)
    pair_ids = jnp.sum(
        jnp.where(slot_table[None, :] == slot_ids[:, None], assignment[None, :], 0), axis=1
    )
    entry_ids = 2 * pair_ids + seq_index % 2
    entry_table = jnp.arange(pair_lengths.shape[0], dtype=jnp.int32)
    live_len = jnp.sum(
        jnp.where(entry_table[None, :] == entry_ids[:, None], pair_lengths[None, :], 0), axis=1
    )
    position = jnp.arange(row_count, dtype=jnp.int32)
    return position % SEQ < jnp.repeat(live_len, SEQ, total_repeat_length=row_count)


def swiglu_grads(head_grad, gate_vals, up_vals):
    gate_float = gate_vals.astype(jnp.float32)
    up_float = up_vals.astype(jnp.float32)
    sigmoid_gate = jax.nn.sigmoid(gate_float)
    silu_gate = gate_float * sigmoid_gate
    hidden = (silu_gate * up_float).astype(jnp.bfloat16)
    grad_gate = (
        head_grad * up_float * sigmoid_gate * (1.0 + gate_float * (1.0 - sigmoid_gate))
    ).astype(jnp.bfloat16)
    grad_up = (head_grad * silu_gate).astype(jnp.bfloat16)
    return (grad_gate, grad_up, hidden)


def on_device(
    activations, cotangent, gate_saved, up_saved, w_gate, w_up, w_down, assignment, pair_lengths
):
    input_rows, output_grads = (
        lax.all_gather(activations, "row", axis=0, tiled=True),
        lax.all_gather(cotangent, "row", axis=0, tiled=True),
    )
    row_count = input_rows.shape[0]
    batch_id = lax.axis_index("dp")
    live_tokens = live_mask(assignment, pair_lengths, batch_id, row_count)
    masked = jnp.where(live_tokens[:, None], output_grads, jnp.zeros_like(output_grads))
    col_count = lax.axis_size("col")
    head_count = row_count // col_count
    block_term = contract_last(masked, w_down).astype(jnp.bfloat16)
    received = lax.all_to_all(block_term, "col", split_axis=0, concat_axis=0, tiled=True)
    stacked = received.reshape(col_count, head_count, received.shape[1])
    head_grad = jnp.sum(stacked, axis=0, dtype=jnp.float32)
    part_gate, part_up, part_hidden = swiglu_grads(head_grad, gate_saved, up_saved)
    grad_gate, grad_up, hidden = (
        lax.all_gather(part_gate, "col", axis=0, tiled=True),
        lax.all_gather(part_up, "col", axis=0, tiled=True),
        lax.all_gather(part_hidden, "col", axis=0, tiled=True),
    )
    input_grad = lax.psum_scatter(
        (contract_last(grad_gate, w_gate) + contract_last(grad_up, w_up)).astype(jnp.bfloat16),
        "row",
        scatter_dimension=0,
        tiled=True,
    )
    grad_scale = 1.0 / jnp.sqrt(jnp.float32(row_count * lax.axis_size("dp")))
    gate_term = contract_first(input_rows, grad_gate) * grad_scale
    up_term = contract_first(input_rows, grad_up) * grad_scale
    down_term = contract_first(hidden, masked) * grad_scale
    gate_total, up_total, down_total = (
        lax.psum_scatter(
            gate_term.astype(jnp.bfloat16), "dp", scatter_dimension=0, tiled=True
        ).astype(jnp.float32),
        lax.psum_scatter(
            up_term.astype(jnp.bfloat16), "dp", scatter_dimension=0, tiled=True
        ).astype(jnp.float32),
        lax.psum_scatter(
            down_term.astype(jnp.bfloat16), "dp", scatter_dimension=0, tiled=True
        ).astype(jnp.float32),
    )
    return (
        input_grad,
        gate_total.astype(jnp.bfloat16),
        up_total.astype(jnp.bfloat16),
        down_total.astype(jnp.bfloat16),
    )


def solution(mesh):
    return jax.shard_map(
        on_device,
        mesh=mesh,
        in_specs=(
            P(("dp", "row"), "col"),
            P(("dp", "row"), "col"),
            P(("dp", "col"), "row"),
            P(("dp", "col"), "row"),
            P("col", "row"),
            P("col", "row"),
            P("row", "col"),
            P(),
            P(),
        ),
        out_specs=(
            P(("dp", "row"), "col"),
            P(("col", "dp"), "row"),
            P(("col", "dp"), "row"),
            P(("row", "dp"), "col"),
        ),
        check_vma=False,
    )
```

profile of v0, /device:TPU:2, one launch (start us, length us, event | category | flops | bytes accessed | tf_op | source)
XLA Modules:
  0.0 1084.4 jit_solution(2719218604420227594)
XLA Ops:
  7.2 0.0 copy-start
  7.2 0.0 all-gather.6.cloned.1.call-start
  7.2 0.7 all-gather.6.cloned.1.call-update
  7.9 0.0 all-gather.14.cloned.1.call-start
  8.0 0.8 select_reduce_fusion.1
  8.8 0.8 select_reduce_fusion
  9.7 0.6 fusion.18
  10.3 3.3 fusion.10
  13.6 32.0 %all-gather.6.cloned.1.call-done = bf16[1024,512]{1,0:T(8,128)(2,1)} async-done(((bf16[128,512]{1,0:T(8,128)(2,1)}), bf16[1024,512]{1,0:T(8,128)(2,1)}) %all-gather.6.cloned.1.call-update) | async-done | bytes 1048592 | tf_op jit(solution)/shard_map/all_gather | solution.py:56
  45.6 3.6 convolution_convert_fusion
  49.1 3.0 copy.14
  52.2 95.9 %all_to_all.9 = bf16[32,32,832]{2,1,0:T(8,128)(2,1)S(1)} all-to-all(bf16[32,32,832]{2,1,0:T(8,128)(2,1)S(1)} %bitcast.19), channel_id=1, replica_groups=mesh['dp'=2,'row'=8,'col'=32] {'col'}, dimensions={0} | all-to-all | bytes 3407872 | tf_op jit(solution)/shard_map/all_to_all | solution.py:65
  148.1 0.3 convert_reduce_fusion
  148.4 0.5 copy-done.1
  148.9 0.0 copy-done.2
  148.9 0.7 multiply_convert_fusion.3
  149.6 0.0 all-gather.14.cloned.1.call-update
  149.7 0.0 all-gather.12.cloned.1.call-start
  149.7 0.7 all-gather.12.cloned.1.call-update
  150.4 0.0 all-gather.8.cloned.1.call-start
  150.5 0.5 all-gather.8.cloned.1.call-update
  151.0 0.0 all-gather.10.cloned.1.call-start
  151.0 0.5 all-gather.10.cloned.1.call-update
  151.6 0.0 reduce-scatter.11.cloned.1.call-start
  151.6 199.6 %all-gather.14.cloned.1.call-done = bf16[1024,832]{1,0:T(8,128)(2,1)} async-done(((bf16[32,832]{1,0:T(8,128)(2,1)}), bf16[1024,832]{1,0:T(8,128)(2,1)}) %all-gather.14.cloned.1.call-update) | async-done | bytes 1703952 | tf_op jit(solution)/shard_map/all_gather | solution.py:72
  351.2 3.5 multiply_convert_fusion
  354.8 0.0 reduce-scatter.11.cloned.1.call-update
  354.8 0.0 reduce-scatter.7.cloned.1.call-start
  354.8 45.7 %all-gather.12.cloned.1.call-done = bf16[1024,512]{1,0:T(8,128)(2,1)} async-done(((bf16[128,512]{1,0:T(8,128)(2,1)}), bf16[1024,512]{1,0:T(8,128)(2,1)}) %all-gather.12.cloned.1.call-update) | async-done | bytes 1048592 | tf_op jit(solution)/shard_map/all_gather | solution.py:55
  400.5 210.0 %all-gather.8.cloned.1.call-done = bf16[1024,832]{1,0:T(8,128)(2,1)} async-done(((bf16[32,832]{1,0:T(8,128)(2,1)}), bf16[1024,832]{1,0:T(8,128)(2,1)}) %all-gather.8.cloned.1.call-update) | async-done | bytes 1703952 | tf_op jit(solution)/shard_map/all_gather | solution.py:70
  610.6 3.8 fusion
  614.3 0.0 reduce-scatter.7.cloned.1.call-update
  614.4 0.0 copy-start.6
  614.4 0.0 reduce-scatter.9.cloned.1.call-start
  614.4 222.3 %all-gather.10.cloned.1.call-done = bf16[1024,832]{1,0:T(8,128)(2,1)} async-done(((bf16[32,832]{1,0:T(8,128)(2,1)}), bf16[1024,832]{1,0:T(8,128)(2,1)}) %all-gather.10.cloned.1.call-update) | async-done | bytes 1703952 | tf_op jit(solution)/shard_map/all_gather | solution.py:71
  836.7 3.8 fusion.1
  840.5 0.0 reduce-scatter.9.cloned.1.call-update
  840.6 0.0 reduce-scatter.5.cloned.1.call-start
  840.6 0.0 copy-start.7
  840.6 1.2 fusion.19
  841.9 0.2 copy-done.4
  842.1 0.2 copy-done.7
  842.3 2.2 add_convert_fusion
  844.6 0.0 reduce-scatter.5.cloned.1.call-update
  844.6 76.8 %reduce-scatter.11.cloned.1.call-done = bf16[416,512]{1,0:T(8,128)(2,1)} async-done(((bf16[832,512]{1,0:T(8,128)(2,1)}), bf16[416,512]{1,0:T(8,128)(2,1)}) %reduce-scatter.11.cloned.1.call-update) | async-done | bytes 426000 | tf_op jit(solution)/shard_map/reduce_scatter | solution.py:91
  921.4 60.5 %reduce-scatter.7.cloned.1.call-done = bf16[256,832]{0,1:T(8,128)(2,1)} async-done(((bf16[512,832]{0,1:T(8,128)(2,1)}), bf16[256,832]{0,1:T(8,128)(2,1)}) %reduce-scatter.7.cloned.1.call-update) | async-done | bytes 426000 | tf_op jit(solution)/shard_map/reduce_scatter | solution.py:85
  981.9 60.6 %reduce-scatter.9.cloned.1.call-done = bf16[256,832]{0,1:T(8,128)(2,1)} async-done(((bf16[512,832]{0,1:T(8,128)(2,1)}), bf16[256,832]{0,1:T(8,128)(2,1)}) %reduce-scatter.9.cloned.1.call-update) | async-done | bytes 426000 | tf_op jit(solution)/shard_map/reduce_scatter | solution.py:88
  1042.5 35.4 %reduce-scatter.5.cloned.1.call-done = bf16[128,512]{1,0:T(8,128)(2,1)} async-done(((bf16[1024,512]{1,0:T(8,128)(2,1)}), bf16[128,512]{1,0:T(8,128)(2,1)}) %reduce-scatter.5.cloned.1.call-update) | async-done | bytes 131088 | tf_op jit(solution)/shard_map/reduce_scatter | solution.py:74
  (11 shorter events, 0.0 us)
Async XLA Ops:
  7.2 38.4 %copy-start = (bf16[832,512]{1,0:T(8,128)(2,1)S(1)}, bf16[832,512]{1,0:T(8,128)(2,1)}, u32[]{:S(2)}) copy-start(bf16[832,512]{1,0:T(8,128)(2,1)} %param.17) | copy-start | bytes 2555908
  7.2 38.4 %all-gather.6.cloned.1.call-start = ((), (), s32[]{:S(2)}) async-start(), calls=%async_computation.5 | async-start | bytes 1179648 | tf_op jit(solution)/shard_map/all_gather | solution.py:56
  7.9 343.3 %all-gather.14.cloned.1.call-start = ((), (), s32[]{:S(2)}) async-start(), calls=%async_computation.12 | async-start | bytes 1892352 | tf_op jit(solution)/shard_map/all_gather | solution.py:72
  148.1 0.8 copy-start.1
  148.1 0.8 copy-start.2
  148.1 203.1 %copy-start.5 = (bf16[1024,512]{1,0:T(8,128)(2,1)S(1)}, bf16[1024,512]{1,0:T(8,128)(2,1)}, u32[]{:S(2)}) copy-start(bf16[1024,512]{1,0:T(8,128)(2,1)} %all-gather.6.cloned.1.call-done) | copy-start | bytes 3145732
  149.7 250.9 %all-gather.12.cloned.1.call-start = ((), (), s32[]{:S(2)}) async-start(), calls=%async_computation.9 | async-start | bytes 1179648 | tf_op jit(solution)/shard_map/all_gather | solution.py:55
  150.4 460.2 %all-gather.8.cloned.1.call-start = ((), (), s32[]{:S(2)}) async-start(), calls=%async_computation.6 | async-start | bytes 1892352 | tf_op jit(solution)/shard_map/all_gather | solution.py:70
  151.0 685.7 %all-gather.10.cloned.1.call-start = ((), (), s32[]{:S(2)}) async-start(), calls=%async_computation.7 | async-start | bytes 1892352 | tf_op jit(solution)/shard_map/all_gather | solution.py:71
  151.6 769.8 %reduce-scatter.11.cloned.1.call-start = ((), (), s32[]{:S(2)}) async-start(), calls=%async_computation.13 | async-start | bytes 1277952 | tf_op jit(solution)/shard_map/reduce_scatter | solution.py:91
  354.8 627.1 %reduce-scatter.7.cloned.1.call-start = ((), (), s32[]{:S(2)}) async-start(), calls=%async_computation.10 | async-start | bytes 1277952 | tf_op jit(solution)/shard_map/reduce_scatter | solution.py:85
  614.4 226.2 %copy-start.3 = (bf16[1024,832]{1,0:T(8,128)(2,1)S(1)}, bf16[1024,832]{1,0:T(8,128)(2,1)}, u32[]{:S(2)}) copy-start(bf16[1024,832]{1,0:T(8,128)(2,1)} %all-gather.8.cloned.1.call-done) | copy-start | bytes 5111812
  614.4 226.2 %copy-start.6 = (bf16[512,832]{0,1:T(8,128)(2,1)S(1)}, bf16[512,832]{0,1:T(8,128)(2,1)}, u32[]{:S(2)}) copy-start(bf16[512,832]{0,1:T(8,128)(2,1)} %param.15) | copy-start | bytes 2555908
  614.4 428.1 %reduce-scatter.9.cloned.1.call-start = ((), (), s32[]{:S(2)}) async-start(), calls=%async_computation.11 | async-start | bytes 1277952 | tf_op jit(solution)/shard_map/reduce_scatter | solution.py:88
  840.6 237.3 %reduce-scatter.5.cloned.1.call-start = ((), (), s32[]{:S(2)}) async-start(), calls=%async_computation.8 | async-start | bytes 1179648 | tf_op jit(solution)/shard_map/reduce_scatter | solution.py:74
  840.6 1.5 copy-start.4
  840.6 1.7 copy-start.7
Sparse Core Ops, SparseCore 0:
  10.1 35.3 all-gather.5
  149.8 201.3 all-gather.13
  353.4 47.0 all-gather.11
  403.0 207.4 all-gather.7
  613.1 223.6 all-gather.9
  840.0 81.3 reduce-scatter.10
  924.8 57.0 reduce-scatter.6
  985.3 57.1 reduce-scatter.8
  1045.9 31.9 reduce-scatter.4
where the time goes:
time: 1080 us
  waiting for transfers between devices  945 us (88%)
  blocking collectives  95.9 us (9%)
  matrix products  18.2 us (2%)
  between operations  13.9 us (1%)
    all_gather x1, waiting for transfers between devices, on_device(): lax.all_gather(part_up, 'col', axis=0, tiled=True)  222 us
    all_gather x1, waiting for transfers between devices, on_device(): lax.all_gather(part_gate, 'col', axis=0, tiled=True)  210 us
    all_gather x1, waiting for transfers between devices, on_device(): lax.all_gather(part_hidden, 'col', axis=0, tiled=True)  200 us
    all_to_all x1, blocking collectives, on_device(): lax.all_to_all(block_term, 'col', split_axis=0, concat_axis=0, tiled=True)  95.9 us
    reduce_scatter x1, waiting for transfers between devices, on_device(): lax.psum_scatter(down_term.astype(jnp.bfloat16), 'dp', scatter_dimension=...  76.8 us
    reduce_scatter x1, waiting for transfers between devices, on_device(): lax.psum_scatter(up_term.astype(jnp.bfloat16), 'dp', scatter_dimension=0,...  60.6 us
    reduce_scatter x1, waiting for transfers between devices, on_device(): lax.psum_scatter(gate_term.astype(jnp.bfloat16), 'dp', scatter_dimension=...  60.5 us
    all_gather x1, waiting for transfers between devices, on_device(): lax.all_gather(activations, 'row', axis=0, tiled=True)  45.7 us
  transfers between devices with their start and end apart: 9, of which 9 were waited for; matrix products, arithmetic and copies ran while one was open for 2% of the time, Pallas kernels for 0%

commit v1 on v0

--- a/solution.py
+++ b/solution.py
@@ -4,6 +4,13 @@
 from jax.sharding import PartitionSpec as P
 
 SEQ = 256
+
+
+def all_by_exchange(value, name, dim):
+    devices = lax.axis_size(name)
+    shards = jnp.stack([value for _ in range(devices)])
+    shards = lax.all_to_all(shards, name, split_axis=0, concat_axis=0)
+    return jnp.concatenate(shards, axis=dim)
 
 
 def contract_last(left, right):
@@ -68,7 +75,7 @@
     part_gate, part_up, part_hidden = swiglu_grads(head_grad, gate_saved, up_saved)
     grad_gate, grad_up, hidden = (
         lax.all_gather(part_gate, "col", axis=0, tiled=True),
-        lax.all_gather(part_up, "col", axis=0, tiled=True),
+        all_by_exchange(part_up, "col", 0),
         lax.all_gather(part_hidden, "col", axis=0, tiled=True),
     )
     input_grad = lax.psum_scatter(

time: 1080 us -> 872 us (0.81)
  waiting for transfers between devices: 945 us -> 721 us
    all_gather x1 -> x0, waiting for transfers between devices: 222 us -> none  [on_device(): lax.all_gather(part_up, 'col', axis=0, tiled=True)]
    all_gather x1, waiting for transfers between devices: 200 us -> 211 us  [on_device(): lax.all_gather(part_hidden, 'col', axis=0, tiled=True)]
  transfers between devices with their start and end apart: 9 -> 9, of which waited for: 9 -> 8; matrix products, arithmetic and copies ran while one was open for 2% -> 3% of each run, Pallas kernels for 0% -> 0%
where the time goes in v1:
time: 872 us; the launch traced here: 871 us
  waiting for transfers between devices  721 us (83%)
  blocking collectives  95.9 us (11%)
  matrix products  19.6 us (2%)
  between operations  14.2 us (2%)
  starting transfers between devices  8.77 us (1%)
    all_gather x1, waiting for transfers between devices, on_device(): lax.all_gather(part_hidden, 'col', axis=0, tiled=True)  211 us
    all_gather x1, waiting for transfers between devices, on_device(): lax.all_gather(part_gate, 'col', axis=0, tiled=True)  210 us
    all_to_all x1, blocking collectives, on_device(): lax.all_to_all(block_term, 'col', split_axis=0, concat_axis=0, tiled=True)  95.9 us
    reduce_scatter x1, waiting for transfers between devices, on_device(): lax.psum_scatter(down_term.astype(jnp.bfloat16), 'dp', scatter_dimension=...  72.3 us
    reduce_scatter x1, waiting for transfers between devices, on_device(): lax.psum_scatter(up_term.astype(jnp.bfloat16), 'dp', scatter_dimension=0,...  60.6 us
    reduce_scatter x1, waiting for transfers between devices, on_device(): lax.psum_scatter(gate_term.astype(jnp.bfloat16), 'dp', scatter_dimension=...  60.4 us
    all_gather x1, waiting for transfers between devices, on_device(): lax.all_gather(activations, 'row', axis=0, tiled=True)  37.7 us
    reduce_scatter x1, waiting for transfers between devices, on_device(): lax.psum_scatter((contract_last(grad_gate, w_gate) + contract_last(grad_u...  35.3 us
  transfers between devices with their start and end apart: 9, of which 8 were waited for; matrix products, arithmetic and copies ran while one was open for 3% of the time, Pallas kernels for 0%

profile of v1, /device:TPU:2, one launch (start us, length us, event | category | flops | bytes accessed | tf_op | source)
XLA Modules:
  0.0 871.3 jit_solution(2708116155343189600)
XLA Ops:
  7.2 0.0 copy-start
  7.2 0.0 all-gather.5.cloned.1.call-start
  7.2 0.7 all-gather.5.cloned.1.call-update
  7.9 0.0 all-gather.11.cloned.1.call-start
  8.0 0.8 select_reduce_fusion.1
  8.8 0.8 select_reduce_fusion
  9.7 0.6 fusion.18
  10.3 3.3 fusion.10
  13.6 32.0 %all-gather.5.cloned.1.call-done = bf16[1024,512]{1,0:T(8,128)(2,1)} async-done(((bf16[128,512]{1,0:T(8,128)(2,1)}), bf16[1024,512]{1,0:T(8,128)(2,1)}) %all-gather.5.cloned.1.call-update) | async-done | bytes 1048592 | tf_op jit(solution)/shard_map/all_gather | solution.py:63
  45.6 0.0 copy-done
  45.6 3.6 convolution_convert_fusion
  49.2 3.0 copy.14
  52.2 95.9 %all_to_all.14 = bf16[32,32,832]{2,1,0:T(8,128)(2,1)S(1)} all-to-all(bf16[32,32,832]{2,1,0:T(8,128)(2,1)S(1)} %bitcast.20), channel_id=1, replica_groups=mesh['dp'=2,'row'=8,'col'=32] {'col'}, dimensions={0} | all-to-all | bytes 3407872 | tf_op jit(solution)/shard_map/all_to_all | solution.py:72
  148.1 0.3 convert_reduce_fusion
  148.4 0.5 copy-done.1
  148.9 0.0 copy-done.2
  148.9 0.7 multiply_convert_fusion.3
  149.7 0.0 all-gather.11.cloned.1.call-update
  149.7 0.0 all-gather.9.cloned.1.call-start
  149.7 0.7 all-gather.9.cloned.1.call-update
  150.4 1.4 stack.2
  151.8 8.4 all-to-all-start.1
  160.3 0.0 all-gather.7.cloned.1.call-start
  160.3 0.5 all-gather.7.cloned.1.call-update
  160.9 0.0 reduce-scatter.11.cloned.1.call-start
  160.9 210.9 %all-gather.11.cloned.1.call-done = bf16[1024,832]{1,0:T(8,128)(2,1)} async-done(((bf16[32,832]{1,0:T(8,128)(2,1)}), bf16[1024,832]{1,0:T(8,128)(2,1)}) %all-gather.11.cloned.1.call-update) | async-done | bytes 1703952 | tf_op jit(solution)/shard_map/all_gather | solution.py:79
  371.8 3.9 multiply_convert_fusion
  375.7 0.0 reduce-scatter.11.cloned.1.call-update
  375.7 0.0 reduce-scatter.7.cloned.1.call-start
  375.8 37.7 %all-gather.9.cloned.1.call-done = bf16[1024,512]{1,0:T(8,128)(2,1)} async-done(((bf16[128,512]{1,0:T(8,128)(2,1)}), bf16[1024,512]{1,0:T(8,128)(2,1)}) %all-gather.9.cloned.1.call-update) | async-done | bytes 1048592 | tf_op jit(solution)/shard_map/all_gather | solution.py:62
  413.5 210.0 %all-gather.7.cloned.1.call-done = bf16[1024,832]{1,0:T(8,128)(2,1)} async-done(((bf16[32,832]{1,0:T(8,128)(2,1)}), bf16[1024,832]{1,0:T(8,128)(2,1)}) %all-gather.7.cloned.1.call-update) | async-done | bytes 1703952 | tf_op jit(solution)/shard_map/all_gather | solution.py:77
  623.5 3.8 fusion
  627.3 0.0 reduce-scatter.7.cloned.1.call-update
  627.3 0.0 reduce-scatter.9.cloned.1.call-start
  627.4 0.0 all-to-all-done.1
  627.4 0.0 copy-start.3
  627.4 3.3 fusion.1
  630.7 0.0 reduce-scatter.9.cloned.1.call-update
  630.8 0.0 reduce-scatter.5.cloned.1.call-start
  630.8 0.0 copy-start.4
  630.8 2.8 fusion.19
  633.6 0.0 copy-done.4
  633.7 2.2 add_convert_fusion
  635.9 0.0 reduce-scatter.5.cloned.1.call-update
  635.9 72.3 %reduce-scatter.11.cloned.1.call-done = bf16[416,512]{1,0:T(8,128)(2,1)} async-done(((bf16[832,512]{1,0:T(8,128)(2,1)}), bf16[416,512]{1,0:T(8,128)(2,1)}) %reduce-scatter.11.cloned.1.call-update) | async-done | bytes 426000 | tf_op jit(solution)/shard_map/reduce_scatter | solution.py:98
  708.2 60.4 %reduce-scatter.7.cloned.1.call-done = bf16[256,832]{0,1:T(8,128)(2,1)} async-done(((bf16[512,832]{0,1:T(8,128)(2,1)}), bf16[256,832]{0,1:T(8,128)(2,1)}) %reduce-scatter.7.cloned.1.call-update) | async-done | bytes 426000 | tf_op jit(solution)/shard_map/reduce_scatter | solution.py:92
  768.5 60.6 %reduce-scatter.9.cloned.1.call-done = bf16[256,832]{0,1:T(8,128)(2,1)} async-done(((bf16[512,832]{0,1:T(8,128)(2,1)}), bf16[256,832]{0,1:T(8,128)(2,1)}) %reduce-scatter.9.cloned.1.call-update) | async-done | bytes 426000 | tf_op jit(solution)/shard_map/reduce_scatter | solution.py:95
  829.2 35.3 %reduce-scatter.5.cloned.1.call-done = bf16[128,512]{1,0:T(8,128)(2,1)} async-done(((bf16[1024,512]{1,0:T(8,128)(2,1)}), bf16[128,512]{1,0:T(8,128)(2,1)}) %reduce-scatter.5.cloned.1.call-update) | async-done | bytes 131088 | tf_op jit(solution)/shard_map/reduce_scatter | solution.py:81
  (5 shorter events, 0.0 us)
Async XLA Ops:
  7.2 38.4 %copy-start = (bf16[832,512]{1,0:T(8,128)(2,1)S(1)}, bf16[832,512]{1,0:T(8,128)(2,1)}, u32[]{:S(2)}) copy-start(bf16[832,512]{1,0:T(8,128)(2,1)} %param.17) | copy-start | bytes 2555908
  7.2 38.4 %all-gather.5.cloned.1.call-start = ((), (), s32[]{:S(2)}) async-start(), calls=%async_computation.6 | async-start | bytes 1179648 | tf_op jit(solution)/shard_map/all_gather | solution.py:63
  7.9 363.9 %all-gather.11.cloned.1.call-start = ((), (), s32[]{:S(2)}) async-start(), calls=%async_computation.12 | async-start | bytes 1892352 | tf_op jit(solution)/shard_map/all_gather | solution.py:79
  148.1 0.8 copy-start.1
  148.1 0.8 copy-start.2
  149.7 263.8 %all-gather.9.cloned.1.call-start = ((), (), s32[]{:S(2)}) async-start(), calls=%async_computation.9 | async-start | bytes 1179648 | tf_op jit(solution)/shard_map/all_gather | solution.py:62
  151.8 475.6 %all-to-all-start.1 = ((bf16[32,32,832]{2,1,0:T(8,128)(2,1)}), bf16[32,32,832]{2,1,0:T(8,128)(2,1)S(1)}, u32[]{:S(2)}, u32[]{:S(2)}) async-start(bf16[32,32,832]{2,1,0:T(8,128)(2,1)} %stack.2), calls=%async_computation.1 | async-start | bytes 3670016 | tf_op jit(solution)/shard_map/all_to_all | solution.py:12
  160.3 463.3 %all-gather.7.cloned.1.call-start = ((), (), s32[]{:S(2)}) async-start(), calls=%async_computation.7 | async-start | bytes 1892352 | tf_op jit(solution)/shard_map/all_gather | solution.py:77
  160.9 547.3 %reduce-scatter.11.cloned.1.call-start = ((), (), s32[]{:S(2)}) async-start(), calls=%async_computation.13 | async-start | bytes 1277952 | tf_op jit(solution)/shard_map/reduce_scatter | solution.py:98
  375.7 392.8 %reduce-scatter.7.cloned.1.call-start = ((), (), s32[]{:S(2)}) async-start(), calls=%async_computation.10 | async-start | bytes 1277952 | tf_op jit(solution)/shard_map/reduce_scatter | solution.py:92
  627.3 201.8 %reduce-scatter.9.cloned.1.call-start = ((), (), s32[]{:S(2)}) async-start(), calls=%async_computation.11 | async-start | bytes 1277952 | tf_op jit(solution)/shard_map/reduce_scatter | solution.py:95
  627.4 3.4 copy-start.3
  630.8 233.7 %reduce-scatter.5.cloned.1.call-start = ((), (), s32[]{:S(2)}) async-start(), calls=%async_computation.8 | async-start | bytes 1179648 | tf_op jit(solution)/shard_map/reduce_scatter | solution.py:81
  630.8 2.8 copy-start.4
Sparse Core Ops, SparseCore 0:
  10.1 35.3 all-gather.4
  149.8 221.9 all-gather.10
  374.0 39.4 all-gather.8
  416.0 207.4 all-gather.6
  626.8 81.3 reduce-scatter.10
  711.4 57.0 reduce-scatter.6
  771.9 57.1 reduce-scatter.8
  832.5 31.8 reduce-scatter.4
